TPU v7x, 512 devices: a whole 4x4x16 slice. The times are simulated.
512 devices in a mesh: tm: 16 (over z_lo, y), series: 32 (over z_hi, x, core).
Axes of the slice: x: 4, y: 4, z: 16 (z_hi: 4, z_lo: 4; z = z_hi * 4 + z_lo), core: 2. Of those that a mesh axis runs over, the one named last changes fastest.
Arguments:
- inputs: bfloat16 [64, 8192, 512], P('series', 'tm'), may hold values from -6 to 6
- cotangent: bfloat16 [64, 8192, 512], P('series', 'tm'), may hold values from -6 to 6
- taps: int32 [3], replicated, may hold values from 0 to 128, as said below
- weight: float32 [1536, 512], P('series'), may hold values from -0.15625 to 0.15625
- moment_one: float32 [1536, 512], P('series'), may hold values from -10 to 10
- second_moment_state: float32 [1536, 512], P('series'), may hold values from 1 to 100
Outputs:
- grad_input: bfloat16 [64, 8192, 512], P('series', 'tm')
- new_weight: float32 [1536, 512], P('series')
- new_moment_one: float32 [1536, 512], P('series')
- new_moment_two: float32 [1536, 512], P('series')
Inputs may be any that keep to these rules, and one draw needn't show every extreme that they name: taps[0] is 0, taps[2] is 128, and taps[1] lies strictly between them.
All inputs are finite; a program needn't handle non-finite values.
Results may differ from a plain program's by a relative error of at most 0.0045.
Values may be sent and summed in bfloat16 or wider, within the bound.
No kernel may reach another device: no remote copies, remote signals or barrier semaphores. Data moves between devices by JAX's collectives and lax.ppermute only.
A program may use at most 64 MiB of HBM per device.

v0:
```python
import jax
import jax.numpy as jnp
from jax import lax
from jax.sharding import PartitionSpec as P

DILATION_GAP = 64


def passed_along(array, axis, by):
    size = lax.axis_size(axis)
    pairs = [(i, i + by) for i in range(size) if 0 <= i + by < size]
    return lax.ppermute(array, axis, pairs)


def adamw(weight, grad, moment_one, second_moment_state):
    first = 0.9 * moment_one + 0.1 * grad
    second = 0.999 * second_moment_state + 0.001 * grad * grad
    unbiased_one = first / (1.0 - 0.9**10)
    unbiased_two = second / (1.0 - 0.999**10)
    updated = weight - 0.01 * (unbiased_one / (jnp.sqrt(unbiased_two) + 1e-08) + 0.1 * weight)
    return (updated, first, second)


def body(inputs, cotangent, taps, weight, moment_one, second_moment_state):
    series_n, time_n, width = inputs.shape
    tap_count = taps.shape[0]
    receptive_span = (tap_count - 1) * DILATION_GAP
    rows = series_n * time_n
    wide = lax.all_gather(weight.astype(jnp.bfloat16), "series", axis=0, tiled=True)
    earlier = passed_along(inputs[:, time_n - receptive_span :, :], "tm", 1)
    extended = jnp.concatenate([earlier, inputs], 1)
    shifted = [
        lax.dynamic_slice_in_dim(extended, receptive_span - taps[k], time_n, 1)
        for k in range(tap_count)
    ]
    stacked = jnp.concatenate(shifted, 2).reshape(rows, tap_count * width)
    pre = jnp.dot(stacked, wide, preferred_element_type=jnp.float32)
    sig = jax.nn.sigmoid(pre)
    upstream = cotangent.reshape(rows, width)
    dpre_flat = (upstream.astype(jnp.float32) * (sig * (1.0 + pre * (1.0 - sig)))).astype(
        jnp.bfloat16
    )
    dpre = dpre_flat.reshape(series_n, time_n, width)
    ahead = passed_along(dpre[:, :receptive_span, :], "tm", -1)
    later = jnp.concatenate([dpre, ahead], 1)
    result = upstream.astype(jnp.float32)
    for k in range(tap_count):
        moved = lax.dynamic_slice_in_dim(later, taps[k], time_n, 1).reshape(rows, width)
        result = result + lax.dot_general(
            moved,
            wide[k * width : (k + 1) * width],
            (((1,), (1,)), ((), ())),
            preferred_element_type=jnp.float32,
        )
    grad_input = result.astype(jnp.bfloat16).reshape(series_n, time_n, width)
    grad_shard = lax.psum_scatter(
        lax.dot_general(
            stacked, dpre_flat, (((0,), (0,)), ((), ())), preferred_element_type=jnp.float32
        ),
        "series",
        scatter_dimension=0,
        tiled=True,
    )
    grad_shard = lax.psum(grad_shard, "tm")
    new_weight, new_moment_one, new_moment_two = adamw(
        weight, grad_shard, moment_one, second_moment_state
    )
    return (grad_input, new_weight, new_moment_one, new_moment_two)


def solution(mesh):
    in_specs = (
        P("series", "tm", None),
        P("series", "tm", None),
        P(),
        P("series", None),
        P("series", None),
        P("series", None),
    )
    out_specs = (P("series", "tm", None), P("series", None), P("series", None), P("series", None))
    return jax.shard_map(body, mesh=mesh, in_specs=in_specs, out_specs=out_specs, check_vma=False)
```

profile of v0, /device:TPU:2, one launch (start us, length us, event | category | flops | bytes accessed | tf_op | source)
XLA Modules:
  0.0 394.1 jit_solution(17457735593663713182)
XLA Ops:
  7.2 1.5 convert_element_type.18
  8.8 0.0 reduce-scatter.2.cloned.1.call-start
  8.8 1.0 slice.27
  9.8 3.5 collective-permute-start
  13.3 1.4 fusion.14
  18.4 0.5 collective-permute-done
  18.8 1.3 constant_dynamic-update-slice_fusion
  20.1 0.8 constant_dynamic-slice_fusion.2
  20.9 0.3 pad_maximum_fusion
  21.2 69.6 %all-gather.2.cloned.1.call-done = bf16[1536,512]{1,0:T(8,128)(2,1)} async-done(((bf16[48,512]{1,0:T(8,128)(2,1)}), bf16[1536,512]{1,0:T(8,128)(2,1)}) %all-gather.2.cloned.1.call-update) | async-done | bytes 1572880 | tf_op jit(solution)/shard_map/all_gather | solution.py:29
  90.8 4.0 %fusion = bf16[1024,512]{1,0:T(8,128)(2,1)S(1)} fusion(bf16[2,512,512]{2,1,0:T(8,128)(2,1)} %param.7, bf16[1024,1536]{1,0:T(8,128)(2,1)S(1)} %bitcast.22, bf16[1536,512]{1,0:T(8,128)(2,1)} %all-gather.2.cloned.1.call-done), kind=kOutput, calls=%fused_computation.3 | convolution fusion | flops 1615855616 | bytes 6815744 | tf_op jit(solution)/shard_map/dot_general | solution.py:37
  94.8 1.0 copy-done
  95.8 3.5 fusion.15
  99.3 0.0 all-reduce.2.cloned.1.call-start
  99.3 1.1 copy-done.1
  100.5 1.3 collective-permute-start.1
  107.4 5.1 %collective-permute-done.1 = bf16[2,128,512]{2,1,0:T(8,128)(2,1)S(1)} collective-permute-done((bf16[2,128,512]{2,1,0:T(8,128)(2,1)S(1)}, bf16[2,128,512]{2,1,0:T(8,128)(2,1)S(1)}, u32[]{:S(2)}, u32[]{:S(2)}) %collective-permute-start.1) | collective-permute-done | bytes 262176 | tf_op jit(solution)/shard_map/ppermute | solution.py:12
  112.5 3.1 fusion.4
  115.6 0.7 fusion.10
  116.3 2.1 fusion.8
  118.4 106.4 %reduce-scatter.2.cloned.1.call-done = f32[48,512]{1,0:T(8,128)} async-done(((f32[1536,512]{1,0:T(8,128)}), f32[48,512]{1,0:T(8,128)}) %reduce-scatter.2.cloned.1.call-update) | async-done | bytes 98320 | tf_op jit(solution)/shard_map/reduce_scatter | solution.py:56
  224.9 3.8 fusion.3
  228.7 157.2 %all-reduce.2.cloned.1.call-done = f32[48,512]{1,0:T(8,128)} async-done(((f32[48,512]{1,0:T(8,128)}), f32[48,512]{1,0:T(8,128)}) %all-reduce.2.cloned.1.call-update) | async-done | bytes 98320 | tf_op jit(solution)/shard_map/psum | solution.py:64
  385.9 1.6 multiply_subtract_fusion
  (16 shorter events, 0.2 us)
Async XLA Ops:
  7.2 83.6 %all-gather.2.cloned.1.call-start = ((), (), s32[]{:S(2)}) async-start(), calls=%async_computation.1 | async-start | bytes 1622016 | tf_op jit(solution)/shard_map/all_gather | solution.py:29
  8.8 216.0 %reduce-scatter.2.cloned.1.call-start = ((), (), s32[]{:S(2)}) async-start(), calls=%async_computation.2 | async-start | bytes 3244032 | tf_op jit(solution)/shard_map/reduce_scatter | solution.py:56
  9.8 9.0 %collective-permute-start = (bf16[2,128,512]{2,1,0:T(8,128)(2,1)S(1)}, bf16[2,128,512]{2,1,0:T(8,128)(2,1)S(1)}, u32[]{:S(2)}, u32[]{:S(2)}) collective-permute-start(bf16[2,128,512]{2,1,0:T(8,128)(2,1)S(1)} %slice.27), channel_id=1, source_target_pairs={{0,32},{32,64},{64,96},{96,128},{128,160},{160,192},{192,224},{224... | collective-permute-start | bytes 786440 | tf_op jit(solution)/shard_map/ppermute | solution.py:12
  94.8 1.0 copy-start
  99.3 1.2 copy-start.1
  99.3 286.6 %all-reduce.2.cloned.1.call-start = ((), (), s32[]{:S(2)}) async-start(), calls=%async_computation.3 | async-start | bytes 196608 | tf_op jit(solution)/shard_map/psum | solution.py:64
  100.5 12.0 %collective-permute-start.1 = (bf16[2,128,512]{2,1,0:T(8,128)(2,1)S(1)}, bf16[2,128,512]{2,1,0:T(8,128)(2,1)S(1)}, u32[]{:S(2)}, u32[]{:S(2)}) collective-permute-start(bf16[2,128,512]{2,1,0:T(8,128)(2,1)S(1)} %slice.35), channel_id=1, source_target_pairs={{32,0},{64,32},{96,64},{128,96},{160,128},{192,160},{224,192},{256... | collective-permute-start | bytes 786440 | tf_op jit(solution)/shard_map/ppermute | solution.py:12
  107.4 8.2 %copy-start.2 = (bf16[1536,512]{1,0:T(8,128)(2,1)S(1)}, bf16[1536,512]{1,0:T(8,128)(2,1)}, u32[]{:S(2)}) copy-start(bf16[1536,512]{1,0:T(8,128)(2,1)} %all-gather.2.cloned.1.call-done) | copy-start | bytes 4718596
  224.8 161.1 %copy-start.3 = (f32[48,512]{1,0:T(8,128)S(1)}, f32[48,512]{1,0:T(8,128)}, u32[]{:S(2)}) copy-start(f32[48,512]{1,0:T(8,128)} %param.9) | copy-start | bytes 294916
  224.8 161.1 %copy-start.4 = (f32[48,512]{1,0:T(8,128)S(1)}, f32[48,512]{1,0:T(8,128)}, u32[]{:S(2)}) copy-start(f32[48,512]{1,0:T(8,128)} %param.10) | copy-start | bytes 294916
  224.8 161.0 %copy-start.5 = (f32[48,512]{1,0:T(8,128)S(1)}, f32[48,512]{1,0:T(8,128)}, u32[]{:S(2)}) copy-start(f32[48,512]{1,0:T(8,128)} %param.11) | copy-start | bytes 294916
Sparse Core Ops, SparseCore 0:
  11.7 79.0 all-gather.1
  99.4 125.3 reduce-scatter.1
  228.0 157.8 all-reduce.1
where the time goes:
time: 395 us; the launch traced here: 394 us
  waiting for transfers between devices  339 us (86%)
  between operations  23.1 us (6%)
  matrix products  14.2 us (4%)
  local copies, waits for them, and re-layouts  6.59 us (2%)
  other arithmetic  6.47 us (2%)
  starting transfers between devices  4.91 us (1%)
    psum x1, waiting for transfers between devices, body(): grad_shard = lax.psum(grad_shard, 'tm')  157 us
    reduce_scatter x1, waiting for transfers between devices, body(): lax.psum_scatter(lax.dot_general(stacked, dpre_flat, (((0,), (0,)), ((),...  106 us
    all_gather x1, waiting for transfers between devices, body(): lax.all_gather(weight.astype(jnp.bfloat16), 'series', axis=0, tiled=True)  69.6 us
  transfers between devices with their start and end apart: 5, of which 5 were waited for; matrix products, arithmetic and copies ran while one was open for 4% of the time, Pallas kernels for 0%

commit v1 on v0

--- a/solution.py
+++ b/solution.py
@@ -26,7 +26,12 @@
     tap_count = taps.shape[0]
     receptive_span = (tap_count - 1) * DILATION_GAP
     rows = series_n * time_n
-    wide = lax.all_gather(weight.astype(jnp.bfloat16), "series", axis=0, tiled=True)
+    wide = jnp.concatenate(
+        lax.all_to_all(
+            jnp.stack([weight.astype(jnp.bfloat16)] * lax.axis_size("series")), "series", 0, 0
+        ),
+        axis=0,
+    )
     earlier = passed_along(inputs[:, time_n - receptive_span :, :], "tm", 1)
     extended = jnp.concatenate([earlier, inputs], 1)
     shifted = [

time: 395 us -> 412 us (1.043)
  starting transfers between devices: 4.91 us -> 23.2 us
    all_gather x1 -> x0, waiting for transfers between devices: 69.6 us -> none  [body(): lax.all_gather(weight.astype(jnp.bfloat16), 'series', axis=0, tiled=True)]
    all_to_all x0 -> x1, waiting for transfers between devices: none -> 65.3 us  [body(): lax.all_to_all(jnp.stack([weight.astype(jnp.bfloat16)] * lax.axis_size('s...]
    all_to_all x0 -> x1, starting transfers between devices: none -> 18.4 us  [body(): lax.all_to_all(jnp.stack([weight.astype(jnp.bfloat16)] * lax.axis_size('s...]
    reduce_scatter x1, waiting for transfers between devices: 106 us -> 114 us  [body(): lax.psum_scatter(lax.dot_general(stacked, dpre_flat, (((0,), (0,)), ((),...]
  transfers between devices with their start and end apart: 5 -> 5, of which waited for: 5 -> 5; matrix products, arithmetic and copies ran while one was open for 4% -> 3% of each run, Pallas kernels for 0% -> 0%
where the time goes in v1:
time: 412 us
  waiting for transfers between devices  339 us (82%)
  between operations  23.9 us (6%)
  starting transfers between devices  23.2 us (6%)
  matrix products  15.3 us (4%)
  other arithmetic  7.38 us (2%)
    psum x1, waiting for transfers between devices, body(): grad_shard = lax.psum(grad_shard, 'tm')  157 us
    reduce_scatter x1, waiting for transfers between devices, body(): lax.psum_scatter(lax.dot_general(stacked, dpre_flat, (((0,), (0,)), ((),...  114 us
    all_to_all x1, waiting for transfers between devices, body(): lax.all_to_all(jnp.stack([weight.astype(jnp.bfloat16)] * lax.axis_size('s...  65.3 us
    all_to_all x1, starting transfers between devices, body(): lax.all_to_all(jnp.stack([weight.astype(jnp.bfloat16)] * lax.axis_size('s...  18.4 us
  transfers between devices with their start and end apart: 5, of which 5 were waited for; matrix products, arithmetic and copies ran while one was open for 3% of the time, Pallas kernels for 0%

profile of v1, /device:TPU:2, one launch (start us, length us, event | category | flops | bytes accessed | tf_op | source)
XLA Modules:
  0.0 411.5 jit_solution(4677909792772582813)
XLA Ops:
  7.2 0.9 convert_element_type.18
  8.1 1.3 stack.2
  9.4 18.4 %all-to-all-start = ((bf16[32,48,512]{2,1,0:T(8,128)(2,1)}), bf16[32,48,512]{2,1,0:T(8,128)(2,1)S(1)}, u32[]{:S(2)}, u32[]{:S(2)}) async-start(bf16[32,48,512]{2,1,0:T(8,128)(2,1)} %stack.2), calls=%async_computation | async-start | bytes 3145728 | tf_op jit(solution)/shard_map/all_to_all | solution.py:30
  27.8 0.0 reduce-scatter.2.cloned.1.call-start
  27.9 3.5 collective-permute-start
  31.4 0.6 fusion.14
  35.9 1.4 collective-permute-done
  37.2 0.1 constant_dynamic-update-slice_fusion
  37.3 0.8 constant_dynamic-slice_fusion.2
  38.1 1.8 pad_maximum_fusion
  39.9 65.3 %all-to-all-done = bf16[32,48,512]{2,1,0:T(8,128)(2,1)S(1)} async-done(((bf16[32,48,512]{2,1,0:T(8,128)(2,1)}), bf16[32,48,512]{2,1,0:T(8,128)(2,1)S(1)}, u32[]{:S(2)}, u32[]{:S(2)}) %all-to-all-start) | async-done | bytes 1572896 | tf_op jit(solution)/shard_map/all_to_all | solution.py:30
  105.2 5.1 %fusion = bf16[1024,512]{1,0:T(8,128)(2,1)S(1)} fusion(bf16[2,512,512]{2,1,0:T(8,128)(2,1)} %param.7, bf16[1024,1536]{1,0:T(8,128)(2,1)} %bitcast.27, bf16[1536,512]{1,0:T(8,128)(2,1)S(1)} %bitcast.20), kind=kOutput, calls=%fused_computation.3 | convolution fusion | flops 1615855616 | bytes 6815744 | tf_op jit(solution)/shard_map/dot_general | solution.py:42
  110.4 3.5 fusion.15
  113.9 0.0 reduce-scatter.2.cloned.1.call-update
  113.9 0.0 all-reduce.2.cloned.1.call-start
  114.0 1.3 collective-permute-start.1
  121.1 1.1 collective-permute-done.1
  122.2 3.1 fusion.4
  125.3 0.7 fusion.10
  126.1 2.1 fusion.8
  128.2 114.0 %reduce-scatter.2.cloned.1.call-done = f32[48,512]{1,0:T(8,128)} async-done(((f32[1536,512]{1,0:T(8,128)}), f32[48,512]{1,0:T(8,128)}) %reduce-scatter.2.cloned.1.call-update) | async-done | bytes 98320 | tf_op jit(solution)/shard_map/reduce_scatter | solution.py:61
  242.2 3.8 fusion.3
  246.0 157.1 %all-reduce.2.cloned.1.call-done = f32[48,512]{1,0:T(8,128)} async-done(((f32[48,512]{1,0:T(8,128)}), f32[48,512]{1,0:T(8,128)}) %all-reduce.2.cloned.1.call-update) | async-done | bytes 98320 | tf_op jit(solution)/shard_map/psum | solution.py:69
  403.0 1.6 multiply_subtract_fusion
  (20 shorter events, 0.1 us)
Async XLA Ops:
  8.1 19.8 %copy-start.3 = (bf16[2,512,512]{2,1,0:T(8,128)(2,1)S(1)}, bf16[2,512,512]{2,1,0:T(8,128)(2,1)}, u32[]{:S(2)}) copy-start(bf16[2,512,512]{2,1,0:T(8,128)(2,1)} %param.6) | copy-start | bytes 3145732
  9.4 22.0 %copy-start.7 = (s32[3]{0:T(128)S(1)}, s32[3]{0:T(128)}, u32[]{:S(2)}) copy-start(s32[3]{0:T(128)} %param.8) | copy-start | bytes 40
  9.4 95.8 %all-to-all-start = ((bf16[32,48,512]{2,1,0:T(8,128)(2,1)}), bf16[32,48,512]{2,1,0:T(8,128)(2,1)S(1)}, u32[]{:S(2)}, u32[]{:S(2)}) async-start(bf16[32,48,512]{2,1,0:T(8,128)(2,1)} %stack.2), calls=%async_computation | async-start | bytes 3145728 | tf_op jit(solution)/shard_map/all_to_all | solution.py:30
  27.8 214.3 %reduce-scatter.2.cloned.1.call-start = ((), (), s32[]{:S(2)}) async-start(), calls=%async_computation.2 | async-start | bytes 3244032 | tf_op jit(solution)/shard_map/reduce_scatter | solution.py:61
  27.9 9.3 %collective-permute-start = (bf16[2,128,512]{2,1,0:T(8,128)(2,1)S(1)}, bf16[2,128,512]{2,1,0:T(8,128)(2,1)S(1)}, u32[]{:S(2)}, u32[]{:S(2)}) collective-permute-start(bf16[2,128,512]{2,1,0:T(8,128)(2,1)S(1)} %slice.27), channel_id=1, source_target_pairs={{0,32},{32,64},{64,96},{96,128},{128,160},{160,192},{192,224},{224... | collective-permute-start | bytes 786440 | tf_op jit(solution)/shard_map/ppermute | solution.py:12
  105.2 5.2 %copy-start = (bf16[32,48,512]{2,1,0:T(8,128)(2,1)}, bf16[32,48,512]{2,1,0:T(8,128)(2,1)S(1)}, u32[]{:S(2)}) copy-start(bf16[32,48,512]{2,1,0:T(8,128)(2,1)S(1)} %all-to-all-done) | copy-start | bytes 4718596
  105.2 5.2 %copy-start.2 = (bf16[2,512,1536]{2,1,0:T(8,128)(2,1)S(1)}, bf16[2,512,1536]{2,1,0:T(8,128)(2,1)}, u32[]{:S(2)}) copy-start(bf16[2,512,1536]{2,1,0:T(8,128)(2,1)} %pad_maximum_fusion) | copy-start | bytes 9437188
  113.9 289.1 %all-reduce.2.cloned.1.call-start = ((), (), s32[]{:S(2)}) async-start(), calls=%async_computation.3 | async-start | bytes 196608 | tf_op jit(solution)/shard_map/psum | solution.py:69
  114.0 8.3 %collective-permute-start.1 = (bf16[2,128,512]{2,1,0:T(8,128)(2,1)S(1)}, bf16[2,128,512]{2,1,0:T(8,128)(2,1)S(1)}, u32[]{:S(2)}, u32[]{:S(2)}) collective-permute-start(bf16[2,128,512]{2,1,0:T(8,128)(2,1)S(1)} %slice.35), channel_id=1, source_target_pairs={{32,0},{64,32},{96,64},{128,96},{160,128},{192,160},{224,192},{256... | collective-permute-start | bytes 786440 | tf_op jit(solution)/shard_map/ppermute | solution.py:12
  121.1 4.2 %copy-start.1 = (bf16[32,48,512]{2,1,0:T(8,128)(2,1)S(1)}, bf16[32,48,512]{2,1,0:T(8,128)(2,1)}, u32[]{:S(2)}) copy-start(bf16[32,48,512]{2,1,0:T(8,128)(2,1)} %copy-done) | copy-start | bytes 4718596
  242.2 160.9 %copy-start.4 = (f32[48,512]{1,0:T(8,128)S(1)}, f32[48,512]{1,0:T(8,128)}, u32[]{:S(2)}) copy-start(f32[48,512]{1,0:T(8,128)} %param.9) | copy-start | bytes 294916
  242.2 160.9 %copy-start.5 = (f32[48,512]{1,0:T(8,128)S(1)}, f32[48,512]{1,0:T(8,128)}, u32[]{:S(2)}) copy-start(f32[48,512]{1,0:T(8,128)} %param.10) | copy-start | bytes 294916
  242.2 160.9 %copy-start.6 = (f32[48,512]{1,0:T(8,128)S(1)}, f32[48,512]{1,0:T(8,128)}, u32[]{:S(2)}) copy-start(f32[48,512]{1,0:T(8,128)} %param.11) | copy-start | bytes 294916
Sparse Core Ops, SparseCore 0:
  114.0 128.0 reduce-scatter.1
  245.3 157.6 all-reduce.1

commit v2 on v0

--- a/solution.py
+++ b/solution.py
@@ -61,7 +61,7 @@
         scatter_dimension=0,
         tiled=True,
     )
-    grad_shard = lax.psum(grad_shard, "tm")
+    grad_shard = jnp.sum(lax.all_gather(grad_shard, "tm"), axis=0)
     new_weight, new_moment_one, new_moment_two = adamw(
         weight, grad_shard, moment_one, second_moment_state
     )

time: 395 us -> 319 us (0.81)
  waiting for transfers between devices: 339 us -> 267 us
    psum x1 -> x0, waiting for transfers between devices: 157 us -> none  [body(): grad_shard = lax.psum(grad_shard, 'tm')]
    all_gather x0 -> x1, waiting for transfers between devices: none -> 69.3 us  [body(): grad_shard = jnp.sum(lax.all_gather(grad_shard, 'tm'), axis=0)]
    reduce_scatter x1, waiting for transfers between devices: 106 us -> 125 us  [body(): lax.psum_scatter(lax.dot_general(stacked, dpre_flat, (((0,), (0,)), ((),...]
  transfers between devices with their start and end apart: 5 -> 5, of which waited for: 5 -> 5; matrix products, arithmetic and copies ran while one was open for 4% -> 3% of each run, Pallas kernels for 0% -> 0%
where the time goes in v2:
time: 319 us
  waiting for transfers between devices  267 us (84%)
  between operations  23.5 us (7%)
  matrix products  10.8 us (3%)
  other arithmetic  7.1 us (2%)
  local copies, waits for them, and re-layouts  5.94 us (2%)
  starting transfers between devices  4.91 us (2%)
    reduce_scatter x1, waiting for transfers between devices, body(): lax.psum_scatter(lax.dot_general(stacked, dpre_flat, (((0,), (0,)), ((),...  125 us
    all_gather x1, waiting for transfers between devices, body(): lax.all_gather(weight.astype(jnp.bfloat16), 'series', axis=0, tiled=True)  69.6 us
    all_gather x1, waiting for transfers between devices, body(): grad_shard = jnp.sum(lax.all_gather(grad_shard, 'tm'), axis=0)  69.3 us
  transfers between devices with their start and end apart: 5, of which 5 were waited for; matrix products, arithmetic and copies ran while one was open for 3% of the time, Pallas kernels for 0%

profile of v2, /device:TPU:2, one launch (start us, length us, event | category | flops | bytes accessed | tf_op | source)
XLA Modules:
  0.0 319.0 jit_solution(15395463038803049072)
XLA Ops:
  7.2 1.5 convert_element_type.18
  8.8 1.0 slice.27
  9.8 3.5 %collective-permute-start = (bf16[2,128,512]{2,1,0:T(8,128)(2,1)S(1)}, bf16[2,128,512]{2,1,0:T(8,128)(2,1)S(1)}, u32[]{:S(2)}, u32[]{:S(2)}) collective-permute-start(bf16[2,128,512]{2,1,0:T(8,128)(2,1)S(1)} %slice.27), channel_id=1, source_target_pairs={{0,32},{32,64},{64,96},{96,128},{128,160},{160,192},{192,224},{224... | collective-permute-start | bytes 786440 | tf_op jit(solution)/shard_map/ppermute | solution.py:12
  13.3 1.4 fusion.14
  18.5 0.3 collective-permute-done
  18.8 1.3 constant_dynamic-update-slice_fusion
  20.1 0.8 constant_dynamic-slice_fusion.2
  20.9 0.3 pad_maximum_fusion
  21.2 69.6 %all-gather.4.cloned.1.call-done = bf16[1536,512]{1,0:T(8,128)(2,1)} async-done(((bf16[48,512]{1,0:T(8,128)(2,1)}), bf16[1536,512]{1,0:T(8,128)(2,1)}) %all-gather.4.cloned.1.call-update) | async-done | bytes 1572880 | tf_op jit(solution)/shard_map/all_gather | solution.py:29
  90.8 4.0 %fusion = bf16[1024,512]{1,0:T(8,128)(2,1)S(1)} fusion(bf16[2,512,512]{2,1,0:T(8,128)(2,1)} %param.7, bf16[1024,1536]{1,0:T(8,128)(2,1)S(1)} %bitcast.23, bf16[1536,512]{1,0:T(8,128)(2,1)} %all-gather.4.cloned.1.call-done), kind=kOutput, calls=%fused_computation.3 | convolution fusion | flops 1615855616 | bytes 6815744 | tf_op jit(solution)/shard_map/dot_general | solution.py:37
  94.8 1.0 copy-done
  95.8 3.5 %fusion.15 = f32[1536,512]{1,0:T(8,128)} fusion(bf16[1024,1536]{1,0:T(8,128)(2,1)S(1)} %bitcast.24, bf16[1024,512]{1,0:T(8,128)(2,1)S(1)} %fusion), kind=kOutput, calls=%fused_computation.31 | convolution fusion | flops 1610612736 | bytes 7340032 | tf_op jit(solution)/shard_map/dot_general | solution.py:57
  99.3 0.0 all-gather.6.cloned.1.call-start
  99.4 125.5 %reduce-scatter.2.cloned.1.call-done = f32[48,512]{1,0:T(8,128)} async-done(((f32[1536,512]{1,0:T(8,128)}), f32[48,512]{1,0:T(8,128)}) %reduce-scatter.2.cloned.1.call-update) | async-done | bytes 98320 | tf_op jit(solution)/shard_map/reduce_scatter | solution.py:56
  224.9 1.3 collective-permute-start.1
  232.0 2.0 collective-permute-done.1
  234.0 3.1 fusion.4
  237.1 0.7 fusion.10
  237.8 0.7 fusion.8
  238.6 0.5 copy-done.3
  239.0 1.8 fusion.3
  240.8 69.3 %all-gather.6.cloned.1.call-done = f32[768,512]{1,0:T(8,128)} async-done(((f32[48,512]{1,0:T(8,128)}), f32[768,512]{1,0:T(8,128)}) %all-gather.6.cloned.1.call-update) | async-done | bytes 1572880 | tf_op jit(solution)/shard_map/all_gather | solution.py:64
  310.2 1.5 reduce_sum.9
  311.7 0.7 multiply_subtract_fusion
  (19 shorter events, 0.2 us)
Async XLA Ops:
  7.2 83.6 %all-gather.4.cloned.1.call-start = ((), (), s32[]{:S(2)}) async-start(), calls=%async_computation.1 | async-start | bytes 1622016 | tf_op jit(solution)/shard_map/all_gather | solution.py:29
  8.8 216.1 %reduce-scatter.2.cloned.1.call-start = ((), (), s32[]{:S(2)}) async-start(), calls=%async_computation.2 | async-start | bytes 3244032 | tf_op jit(solution)/shard_map/reduce_scatter | solution.py:56
  9.8 9.0 %collective-permute-start = (bf16[2,128,512]{2,1,0:T(8,128)(2,1)S(1)}, bf16[2,128,512]{2,1,0:T(8,128)(2,1)S(1)}, u32[]{:S(2)}, u32[]{:S(2)}) collective-permute-start(bf16[2,128,512]{2,1,0:T(8,128)(2,1)S(1)} %slice.27), channel_id=1, source_target_pairs={{0,32},{32,64},{64,96},{96,128},{128,160},{160,192},{192,224},{224... | collective-permute-start | bytes 786440 | tf_op jit(solution)/shard_map/ppermute | solution.py:12
  94.8 1.0 copy-start
  99.3 125.6 %copy-start.1 = (bf16[1024,512]{1,0:T(8,128)(2,1)S(1)}, bf16[1024,512]{1,0:T(8,128)(2,1)}, u32[]{:S(2)}) copy-start(bf16[1024,512]{1,0:T(8,128)(2,1)} %copy-done) | copy-start | bytes 3145732
  99.3 210.9 %all-gather.6.cloned.1.call-start = ((), (), s32[]{:S(2)}) async-start(), calls=%async_computation.3 | async-start | bytes 1671168 | tf_op jit(solution)/shard_map/all_gather | solution.py:64
  224.9 9.1 %collective-permute-start.1 = (bf16[2,128,512]{2,1,0:T(8,128)(2,1)S(1)}, bf16[2,128,512]{2,1,0:T(8,128)(2,1)S(1)}, u32[]{:S(2)}, u32[]{:S(2)}) collective-permute-start(bf16[2,128,512]{2,1,0:T(8,128)(2,1)S(1)} %slice.35), channel_id=1, source_target_pairs={{32,0},{64,32},{96,64},{128,96},{160,128},{192,160},{224,192},{256... | collective-permute-start | bytes 786440 | tf_op jit(solution)/shard_map/ppermute | solution.py:12
  232.0 5.1 %copy-start.2 = (bf16[1536,512]{1,0:T(8,128)(2,1)S(1)}, bf16[1536,512]{1,0:T(8,128)(2,1)}, u32[]{:S(2)}) copy-start(bf16[1536,512]{1,0:T(8,128)(2,1)} %all-gather.4.cloned.1.call-done) | copy-start | bytes 4718596
  237.8 1.2 copy-start.3
  239.0 72.6 %copy-start.4 = (f32[48,512]{1,0:T(8,128)S(1)}, f32[48,512]{1,0:T(8,128)}, u32[]{:S(2)}) copy-start(f32[48,512]{1,0:T(8,128)} %param.9) | copy-start | bytes 294916
  239.0 72.7 %copy-start.5 = (f32[48,512]{1,0:T(8,128)S(1)}, f32[48,512]{1,0:T(8,128)}, u32[]{:S(2)}) copy-start(f32[48,512]{1,0:T(8,128)} %param.10) | copy-start | bytes 294916
  239.0 72.7 %copy-start.6 = (f32[48,512]{1,0:T(8,128)S(1)}, f32[48,512]{1,0:T(8,128)}, u32[]{:S(2)}) copy-start(f32[48,512]{1,0:T(8,128)} %param.11) | copy-start | bytes 294916
Sparse Core Ops, SparseCore 0:
  11.7 79.0 all-gather.3
  99.4 125.3 reduce-scatter.1
  227.1 83.0 all-gather.5
